TPU v7x, 32 devices: a whole 2x2x4 slice. The times are simulated.
32 devices in a mesh: seq: 8 (over z, y), chan: 4 (over x, core).
Axes of the slice: x: 2, y: 2, z: 4, core: 2. Of those that a mesh axis runs over, the one named last changes fastest.
Arguments:
- tokens: bfloat16 [4096, 4096], P('seq', 'chan'), may hold values from -6 to 6
- grad_out: bfloat16 [4096, 4096], P('seq', 'chan'), may hold values from -0.125 to 0.125
- in_weight: bfloat16 [4096, 3, 256], P('seq', None, 'chan'), may hold values from -0.09375 to 0.09375
- out_weight: bfloat16 [4096, 256], P('seq', 'chan'), may hold values from -0.09375 to 0.09375
- conv_out: bfloat16 [4096, 256], P('seq', 'chan'), may hold values from -6 to 6
- residues: float32 [16, 128], P(None, 'chan'), may hold values from -1.5 to 1.5
- decay_length: float32 [16, 128], P(None, 'chan'), may hold values from 8 to 262144
Outputs:
- grad_in_weight: float32 [4096, 3, 256], P('seq', None, 'chan')
- grad_out_weight: float32 [4096, 256], P('seq', 'chan')
All inputs are finite; a program needn't handle non-finite values.
Results may differ from a plain program's by a relative error of at most 0.0041.
Values may be sent and summed in bfloat16 or wider, within the bound.
A program may use at most 64 MiB of HBM per device.

v0:
```python
import math

import jax
import jax.numpy as jnp
from jax import lax
from jax.sharding import PartitionSpec as P

precise = lax.Precision.HIGHEST


def swapped(value, axis, apart):
    mask = 2**apart
    pairs = [(source, source ^ mask) for source in range(lax.axis_size(axis))]
    return lax.ppermute(value, axis, pairs)


def rotate(packed, radians):
    real_part = packed[..., 0, :]
    imag_part = packed[..., 1, :]
    cosine = jnp.cos(radians)
    sine_value = jnp.sin(radians)
    return jnp.stack(
        [real_part * cosine + imag_part * sine_value, imag_part * cosine - real_part * sine_value],
        axis=-2,
    )


def angle_tables(height, breadth, period):
    row_index = jnp.arange(height, dtype=jnp.int32)
    col_index = jnp.arange(breadth, dtype=jnp.int32)
    product = row_index[:, None] * col_index[None, :] % period
    radians = product.astype(jnp.float32) * (2.0 * math.pi / period)
    return (jnp.cos(radians), jnp.sin(radians))


def transform(formula, packed, cosine, sine_table, direction):
    along_cos = jnp.einsum(formula, cosine, packed, precision=precise)
    along_sin = jnp.einsum(formula, sine_table, packed, precision=precise)
    real_part = along_cos[..., 0, :] + direction * along_sin[..., 1, :]
    imag_part = along_cos[..., 1, :] - direction * along_sin[..., 0, :]
    return jnp.stack([real_part, imag_part], axis=-2)


def filter_spectrum(residues, decay_length, low_freq, local_rows, devices_seq):
    period = 2 * local_rows * devices_seq
    sequence = local_rows * devices_seq
    frequency = (
        low_freq[:, None] + 2 * devices_seq * jnp.arange(local_rows, dtype=jnp.int32)[None, :]
    )
    signed_freq = jnp.where(frequency > period // 2, frequency - period, frequency)
    phase_angle = signed_freq.astype(jnp.float32) * (2.0 * math.pi / period)
    parity = 1.0 - 2.0 * (low_freq % 2).astype(jnp.float32)
    inverse_len = 1.0 / decay_length
    decay_rate = jnp.exp(-inverse_len)
    weight = residues * jnp.sqrt(-jnp.expm1(-2.0 * inverse_len))
    remnant = jnp.exp(-inverse_len * sequence)
    half_sine = jnp.sin(0.5 * phase_angle)[None, :, :, None]
    full_sine = jnp.sin(phase_angle)[None, :, :, None]
    real_den = (
        -jnp.expm1(-inverse_len)[:, None, None, :]
        + 2.0 * decay_rate[:, None, None, :] * half_sine * half_sine
    )
    imag_den = decay_rate[:, None, None, :] * full_sine
    numerator = weight[:, None, None, :] * (
        1.0 - remnant[:, None, None, :] * parity[None, :, None, None]
    )
    factor = numerator / (real_den * real_den + imag_den * imag_den)
    return (jnp.sum(factor * real_den, axis=0), jnp.sum(factor * imag_den, axis=0))


def correlate(signal, residues, decay_length):
    local_rows, channels = signal.shape
    devices_seq = lax.axis_size("seq")
    position = lax.axis_index("seq")
    period = 2 * local_rows * devices_seq
    paired = channels // 2
    sections = devices_seq.bit_length() - 1
    packed = signal.reshape(local_rows, paired, 2).transpose(0, 2, 1)
    shifted = rotate(packed, position.astype(jnp.float32) * (math.pi / devices_seq))
    spectral = jnp.stack([packed, shifted], axis=0)
    for section_bit in reversed(range(sections)):
        stride = 1 << section_bit
        partner = swapped(spectral, "seq", section_bit)
        twiddle = (position % stride).astype(jnp.float32) * (math.pi / stride)
        on_upper = position // stride % 2 == 1
        spectral = jnp.where(on_upper, rotate(partner - spectral, twiddle), spectral + partner)
    flipped = jnp.zeros((), jnp.int32)
    for section_bit in range(sections):
        flipped = flipped * 2 + position // (1 << section_bit) % 2
    low_freq = 2 * flipped
    low_freq = low_freq + jnp.arange(2, dtype=jnp.int32)
    offsets = jnp.arange(local_rows, dtype=jnp.int32)
    twiddles = (low_freq[:, None] * offsets[None, :] % period).astype(jnp.float32) * (
        2.0 * math.pi / period
    )
    twiddles = twiddles[:, :, None]
    cosine, sine_table = angle_tables(local_rows, local_rows, local_rows)
    spectrum = transform("km,emrf->ekrf", rotate(spectral, twiddles), cosine, sine_table, 1.0)
    resp_real, resp_imag = filter_spectrum(
        residues, decay_length, low_freq, local_rows, devices_seq
    )
    spec_real = spectrum[:, :, 0, :]
    spec_imag = spectrum[:, :, 1, :]
    weighted = jnp.stack(
        [
            spec_real * resp_real - spec_imag * resp_imag,
            spec_real * resp_imag + spec_imag * resp_real,
        ],
        axis=2,
    )
    returned = rotate(transform("km,emrf->ekrf", weighted, cosine, sine_table, -1.0), -twiddles)
    for section_bit in range(sections):
        stride = 1 << section_bit
        partner = swapped(returned, "seq", section_bit)
        twiddle = (position % stride).astype(jnp.float32) * (math.pi / stride)
        on_upper = position // stride % 2 == 1
        returned = jnp.where(
            on_upper, partner - rotate(returned, -twiddle), returned + rotate(partner, -twiddle)
        )
    result = returned[0] + rotate(
        returned[1], -position.astype(jnp.float32) * (math.pi / devices_seq)
    )
    result = result * (1.0 / period)
    return result.transpose(0, 2, 1).reshape(local_rows, channels)


def local(tokens, grad_out, in_weight, out_weight, conv_out, residues, decay_length):
    local_rows = tokens.shape[0]
    channels = out_weight.shape[1]
    owned_rows = in_weight.shape[0]
    full_tokens, full_grads = (
        lax.all_gather(tokens, "chan", axis=1, tiled=True),
        lax.all_gather(grad_out, "chan", axis=1, tiled=True),
    )
    pieces = (
        lax.all_gather(in_weight, "seq", axis=0, tiled=True),
        lax.all_gather(out_weight, "seq", axis=0, tiled=True),
    )
    piece_rows = pieces[0].shape[0]
    token_cols = full_tokens
    grad_cols = full_grads
    projected = jnp.dot(
        token_cols, pieces[0].reshape(piece_rows, 3 * channels), preferred_element_type=jnp.float32
    )
    upstream = jnp.dot(grad_cols, pieces[1], preferred_element_type=jnp.float32)
    projected, upstream = (projected, upstream)
    streams = projected.astype(jnp.bfloat16).reshape(local_rows, 3, channels)
    gate_first = streams[:, 0].astype(jnp.float32)
    gate_second = streams[:, 1].astype(jnp.float32)
    value_stream = streams[:, 2].astype(jnp.float32)
    conv_value = conv_out.astype(jnp.float32)
    gated = (gate_second * conv_value).astype(jnp.bfloat16)
    grad_second = (upstream * conv_value).astype(jnp.bfloat16)
    grad_conv = upstream * gate_second
    grad_source = correlate(grad_conv, residues, decay_length)
    grad_first = (grad_source * value_stream).astype(jnp.bfloat16)
    grad_value = (grad_source * gate_first).astype(jnp.bfloat16)
    grad_streams = jnp.stack([grad_first, grad_second, grad_value], axis=1).reshape(
        local_rows, 3 * channels
    )
    token_cols = full_tokens
    grad_cols = full_grads
    inward = lax.dot_general(
        token_cols, grad_streams, (((0,), (0,)), ((), ())), preferred_element_type=jnp.float32
    )
    outward = lax.dot_general(
        grad_cols, gated, (((0,), (0,)), ((), ())), preferred_element_type=jnp.float32
    )
    owned = lax.psum_scatter(
        jnp.concatenate([inward, outward], axis=1), "seq", scatter_dimension=0, tiled=True
    )
    grad_in = owned[:, : 3 * channels].reshape(owned_rows, 3, channels)
    grad_proj = owned[:, 3 * channels :]
    return (grad_in, grad_proj)


def solution(mesh):
    return jax.shard_map(
        local,
        mesh=mesh,
        in_specs=(
            P("seq", "chan"),
            P("seq", "chan"),
            P("seq", None, "chan"),
            P("seq", "chan"),
            P("seq", "chan"),
            P(None, "chan"),
            P(None, "chan"),
        ),
        out_specs=(P("seq", None, "chan"), P("seq", "chan")),
        check_vma=False,
    )
```

profile of v0, /device:TPU:0, one launch (start us, length us, event | category | flops | bytes accessed | tf_op | source)
XLA Modules:
  0.0 314.7 jit_solution(13981726833255500663)
XLA Ops:
  7.2 0.7 all-gather.8.cloned.1.call-update
  7.9 0.7 all-gather.6.cloned.1.call-update
  8.6 0.0 all-gather.4.cloned.1.call-start
  8.7 0.7 all-gather.4.cloned.1.call-update
  9.4 0.0 reduce-scatter.2.cloned.1.call-start
  9.7 34.1 %all_gather.13 = bf16[4096,64]{0,1:T(8,128)(2,1)S(1)} all-gather(bf16[512,64]{0,1:T(8,128)(2,1)} %param.10), channel_id=1, replica_groups=mesh['seq'=8,'chan'=4] {'seq'}, dimensions={0}, use_global_device_ids=true | all-gather | bytes 589824 | tf_op jit(solution)/shard_map/all_gather | solution.py:137
  43.8 15.8 %all-gather.8.cloned.1.call-done = bf16[4096,3,64]{0,2,1:T(8,128)(2,1)} async-done(((bf16[512,3,64]{0,2,1:T(8,128)(2,1)}), bf16[4096,3,64]{0,2,1:T(8,128)(2,1)}) %all-gather.8.cloned.1.call-update) | async-done | bytes 1572880 | tf_op jit(solution)/shard_map/all_gather | solution.py:136
  59.6 34.6 %all-gather.6.cloned.1.call-done = bf16[512,4096]{1,0:T(8,128)(2,1)} async-done(((bf16[512,1024]{1,0:T(8,128)(2,1)}), bf16[512,4096]{1,0:T(8,128)(2,1)}) %all-gather.6.cloned.1.call-update) | async-done | bytes 4194320 | tf_op jit(solution)/shard_map/all_gather | solution.py:132
  94.2 4.2 %convolution_convert_fusion = bf16[512,192]{0,1:T(8,128)(2,1)S(1)} fusion(bf16[512,4096]{1,0:T(8,128)(2,1)} %all-gather.6.cloned.1.call-done, bf16[4096,192]{0,1:T(8,128)(2,1)} %bitcast.96), kind=kOutput, calls=%fused_computation.13 | convolution fusion | flops 805404672 | bytes 5963776 | tf_op jit(solution)/shard_map/dot_general | solution.py:142
  98.4 31.8 %all-gather.4.cloned.1.call-done = bf16[512,4096]{1,0:T(8,128)(2,1)} async-done(((bf16[512,1024]{1,0:T(8,128)(2,1)}), bf16[512,4096]{1,0:T(8,128)(2,1)}) %all-gather.4.cloned.1.call-update) | async-done | bytes 4194320 | tf_op jit(solution)/shard_map/all_gather | solution.py:133
  130.2 3.6 %fusion.32 = (bf16[512,1,64]{0,2,1:T(8,128)(2,1)S(1)}, f32[512,64]{0,1:T(8,128)S(1)}) fusion(bf16[512,64]{0,1:T(8,128)(2,1)S(1)} %copy-done, bf16[512,3,64]{0,2,1:T(8,128)(2,1)S(1)} %bitcast.93, bf16[512,4096]{1,0:T(8,128)(2,1)} %all-gather.4.cloned.1.call-done, bf16[4096,64]{0,1:T(8,128)(2,1)S(1)} %all_gather.13), kind=kOutput, calls=%fused_computation.96 | convolution fusion | flops 268599296 | bytes 5046272 | tf_op jit(solution)/shard_map/dot_general | solution.py:145
  133.8 0.1 reshape.244
  134.0 2.5 collective-permute-start
  136.5 0.3 multiply_sine_fusion
  137.0 12.0 %collective-permute-done = f32[2,512,2,32]{1,3,2,0:T(8,128)S(1)} collective-permute-done((f32[2,512,2,32]{1,3,2,0:T(8,128)S(1)}, f32[2,512,2,32]{1,3,2,0:T(8,128)S(1)}, u32[]{:S(2)}, u32[]{:S(2)}) %collective-permute-start) | collective-permute-done | bytes 262176 | tf_op jit(solution)/shard_map/ppermute | solution.py:14
  149.1 0.1 maximum_select_fusion
  149.2 0.6 collective-permute-start.1
  149.9 0.1 subtract_multiply_fusion
  150.0 6.8 %collective-permute-done.1 = f32[2,512,2,32]{1,3,2,0:T(8,128)S(1)} collective-permute-done((f32[2,512,2,32]{1,3,2,0:T(8,128)S(1)}, f32[2,512,2,32]{1,3,2,0:T(8,128)S(1)}, u32[]{:S(2)}, u32[]{:S(2)}) %collective-permute-start.1) | collective-permute-done | bytes 262176 | tf_op jit(solution)/shard_map/ppermute | solution.py:14
  156.8 0.1 fusion.71
  157.0 0.1 maximum_select_fusion.1
  157.1 1.5 collective-permute-start.2
  158.7 1.6 multiply_reduce_fusion
  160.2 3.7 %collective-permute-done.2 = f32[2,512,2,32]{1,3,2,0:T(8,128)S(1)} collective-permute-done((f32[2,512,2,32]{1,3,2,0:T(8,128)S(1)}, f32[2,512,2,32]{1,3,2,0:T(8,128)S(1)}, u32[]{:S(2)}, u32[]{:S(2)}) %collective-permute-start.2) | collective-permute-done | bytes 262176 | tf_op jit(solution)/shard_map/ppermute | solution.py:14
  164.0 0.1 maximum_select_fusion.2
  164.1 4.9 %convolution_bitcast_fusion.4 = f32[2,512,2,32]{1,3,2,0:T(8,128)S(1)} fusion(f32[2,512,1,32]{1,3,2,0:T(8,128)S(1)} %get-tuple-element.12, f32[2,512,1,32]{1,3,2,0:T(8,128)S(1)} %get-tuple-element.11), kind=kOutput, calls=%fused_computation.16 | convolution fusion | flops 406388736 | bytes 524288 | tf_op jit(solution)/shard_map/km,emrf->ekrf/dot_general | solution.py:38
  169.0 4.9 %convolution_bitcast_fusion.5 = f32[2,512,2,32]{1,3,2,0:T(8,128)S(1)} fusion(f32[2,512,1,32]{1,3,2,0:T(8,128)S(1)} %get-tuple-element.12, f32[2,512,1,32]{1,3,2,0:T(8,128)S(1)} %get-tuple-element.11), kind=kOutput, calls=%fused_computation.17 | convolution fusion | flops 406388736 | bytes 524288 | tf_op jit(solution)/shard_map/km,emrf->ekrf/dot_general | solution.py:37
  174.0 0.1 fusion.29
  174.0 5.1 %convolution_bitcast_fusion.2 = f32[2,512,2,32]{1,3,2,0:T(8,128)S(1)} fusion(f32[2,512,1,32]{1,3,2,0:T(8,128)S(1)} %get-tuple-element.8, f32[2,512,1,32]{1,3,2,0:T(8,128)S(1)} %get-tuple-element.7), kind=kOutput, calls=%fused_computation.14 | convolution fusion | flops 406388736 | bytes 524288 | tf_op jit(solution)/shard_map/km,emrf->ekrf/dot_general | solution.py:38
  179.2 4.9 %convolution_bitcast_fusion.3 = f32[2,512,2,32]{1,3,2,0:T(8,128)S(1)} fusion(f32[2,512,1,32]{1,3,2,0:T(8,128)S(1)} %get-tuple-element.8, f32[2,512,1,32]{1,3,2,0:T(8,128)S(1)} %get-tuple-element.7), kind=kOutput, calls=%fused_computation.15 | convolution fusion | flops 406388736 | bytes 524288 | tf_op jit(solution)/shard_map/km,emrf->ekrf/dot_general | solution.py:37
  184.1 0.1 multiply_add_fusion.6
  184.2 1.5 collective-permute-start.3
  185.8 4.9 %collective-permute-done.3 = f32[2,512,2,32]{1,3,2,0:T(8,128)S(1)} collective-permute-done((f32[2,512,2,32]{1,3,2,0:T(8,128)S(1)}, f32[2,512,2,32]{1,3,2,0:T(8,128)S(1)}, u32[]{:S(2)}, u32[]{:S(2)}) %collective-permute-start.3) | collective-permute-done | bytes 262176 | tf_op jit(solution)/shard_map/ppermute | solution.py:14
  190.7 0.1 fusion.19
  190.8 2.0 collective-permute-start.4
  193.3 3.9 %collective-permute-done.4 = f32[2,512,2,32]{1,3,2,0:T(8,128)S(1)} collective-permute-done((f32[2,512,2,32]{1,3,2,0:T(8,128)S(1)}, f32[2,512,2,32]{1,3,2,0:T(8,128)S(1)}, u32[]{:S(2)}, u32[]{:S(2)}) %collective-permute-start.4) | collective-permute-done | bytes 262176 | tf_op jit(solution)/shard_map/ppermute | solution.py:14
  197.3 0.2 fusion.20
  197.5 5.6 %collective-permute-start.5 = (f32[2,512,2,32]{1,3,2,0:T(8,128)S(1)}, f32[2,512,2,32]{1,3,2,0:T(8,128)S(1)}, u32[]{:S(2)}, u32[]{:S(2)}) collective-permute-start(f32[2,512,2,32]{1,3,2,0:T(8,128)S(1)} %fusion.20), channel_id=1, source_target_pairs={{0,16},{4,20},{8,24},{12,28},{16,0},{20,4},{24,8},{28,12},{1,17},{... | collective-permute-start | bytes 786440 | tf_op jit(solution)/shard_map/ppermute | solution.py:14
  203.0 3.0 convolution_bitcast_fusion.1
  206.1 4.3 %collective-permute-done.5 = f32[2,512,2,32]{1,3,2,0:T(8,128)S(1)} collective-permute-done((f32[2,512,2,32]{1,3,2,0:T(8,128)S(1)}, f32[2,512,2,32]{1,3,2,0:T(8,128)S(1)}, u32[]{:S(2)}, u32[]{:S(2)}) %collective-permute-start.5) | collective-permute-done | bytes 262176 | tf_op jit(solution)/shard_map/ppermute | solution.py:14
  210.4 0.1 fusion.21
  210.6 0.1 copy.12
  210.7 0.1 reshape.245
  210.9 3.3 %convolution_bitcast_fusion = f32[4096,192]{0,1:T(8,128)S(1)} fusion(bf16[512,192]{0,1:T(8,128)(2,1)S(1)} %bitcast.91, bf16[512,4096]{1,0:T(8,128)(2,1)} %all-gather.6.cloned.1.call-done), kind=kOutput, calls=%fused_computation | convolution fusion | flops 805306368 | bytes 7536640 | tf_op jit(solution)/shard_map/dot_general | solution.py:163
  214.1 2.2 pad_maximum_fusion
  216.4 88.5 %reduce-scatter.2.cloned.1.call-done = f32[512,256]{0,1:T(8,128)} async-done(((f32[4096,256]{0,1:T(8,128)}), f32[512,256]{0,1:T(8,128)}) %reduce-scatter.2.cloned.1.call-update) | async-done | bytes 524304 | tf_op jit(solution)/shard_map/reduce_scatter | solution.py:169
  304.9 1.6 slice.184
  306.4 1.8 slice.183
  (35 shorter events, 0.7 us)
Async XLA Ops:
  7.2 52.4 %all-gather.8.cloned.1.call-start = ((), (), s32[]{:S(2)}) async-start(), calls=%async_computation.3 | async-start | bytes 1769472 | tf_op jit(solution)/shard_map/all_gather | solution.py:136
  7.9 86.3 %all-gather.6.cloned.1.call-start = ((), (), s32[]{:S(2)}) async-start(), calls=%async_computation.2 | async-start | bytes 5242880 | tf_op jit(solution)/shard_map/all_gather | solution.py:132
  8.6 121.6 %all-gather.4.cloned.1.call-start = ((), (), s32[]{:S(2)}) async-start(), calls=%async_computation.1 | async-start | bytes 5242880 | tf_op jit(solution)/shard_map/all_gather | solution.py:133
  9.4 295.5 %reduce-scatter.2.cloned.1.call-start = ((), (), s32[]{:S(2)}) async-start(), calls=%async_computation.4 | async-start | bytes 4718592 | tf_op jit(solution)/shard_map/reduce_scatter | solution.py:169
  94.1 36.1 %copy-start = (bf16[512,64]{0,1:T(8,128)(2,1)S(1)}, bf16[512,64]{0,1:T(8,128)(2,1)}, u32[]{:S(2)}) copy-start(bf16[512,64]{0,1:T(8,128)(2,1)} %param.11) | copy-start | bytes 196612
  130.2 6.8 %copy-start.1 = (f32[16,32]{1,0:T(8,128)S(1)}, f32[16,32]{1,0:T(8,128)}, u32[]{:S(2)}) copy-start(f32[16,32]{1,0:T(8,128)} %param.12) | copy-start | bytes 6148
  130.2 6.8 %copy-start.2 = (f32[16,32]{1,0:T(8,128)S(1)}, f32[16,32]{1,0:T(8,128)}, u32[]{:S(2)}) copy-start(f32[16,32]{1,0:T(8,128)} %param.13) | copy-start | bytes 6148
  134.0 15.0 %collective-permute-start = (f32[2,512,2,32]{1,3,2,0:T(8,128)S(1)}, f32[2,512,2,32]{1,3,2,0:T(8,128)S(1)}, u32[]{:S(2)}, u32[]{:S(2)}) collective-permute-start(f32[2,512,2,32]{1,3,2,0:T(8,128)S(1)} %pad_maximum_fusion.1), channel_id=1, source_target_pairs={{0,16},{4,20},{8,24},{12,28},{16,0},{20,4},{24,8},{28,12},{1,17},{... | collective-permute-start | bytes 786440 | tf_op jit(solution)/shard_map/ppermute | solution.py:14
  149.2 7.7 %collective-permute-start.1 = (f32[2,512,2,32]{1,3,2,0:T(8,128)S(1)}, f32[2,512,2,32]{1,3,2,0:T(8,128)S(1)}, u32[]{:S(2)}, u32[]{:S(2)}) collective-permute-start(f32[2,512,2,32]{1,3,2,0:T(8,128)S(1)} %maximum_select_fusion), channel_id=1, source_target_pairs={{0,8},{4,12},{8,0},{12,4},{16,24},{20,28},{24,16},{28,20},{1,9},{5... | collective-permute-start | bytes 786440 | tf_op jit(solution)/shard_map/ppermute | solution.py:14
  157.1 6.8 %collective-permute-start.2 = (f32[2,512,2,32]{1,3,2,0:T(8,128)S(1)}, f32[2,512,2,32]{1,3,2,0:T(8,128)S(1)}, u32[]{:S(2)}, u32[]{:S(2)}) collective-permute-start(f32[2,512,2,32]{1,3,2,0:T(8,128)S(1)} %maximum_select_fusion.1), channel_id=1, source_target_pairs={{0,4},{4,0},{8,12},{12,8},{16,20},{20,16},{24,28},{28,24},{1,5},{5... | collective-permute-start | bytes 786440 | tf_op jit(solution)/shard_map/ppermute | solution.py:14
  184.2 6.4 %collective-permute-start.3 = (f32[2,512,2,32]{1,3,2,0:T(8,128)S(1)}, f32[2,512,2,32]{1,3,2,0:T(8,128)S(1)}, u32[]{:S(2)}, u32[]{:S(2)}) collective-permute-start(f32[2,512,2,32]{1,3,2,0:T(8,128)S(1)} %pad_maximum_fusion.4), channel_id=1, source_target_pairs={{0,4},{4,0},{8,12},{12,8},{16,20},{20,16},{24,28},{28,24},{1,5},{5... | collective-permute-start | bytes 786440 | tf_op jit(solution)/shard_map/ppermute | solution.py:14
  190.8 6.4 %collective-permute-start.4 = (f32[2,512,2,32]{1,3,2,0:T(8,128)S(1)}, f32[2,512,2,32]{1,3,2,0:T(8,128)S(1)}, u32[]{:S(2)}, u32[]{:S(2)}) collective-permute-start(f32[2,512,2,32]{1,3,2,0:T(8,128)S(1)} %fusion.19), channel_id=1, source_target_pairs={{0,8},{4,12},{8,0},{12,4},{16,24},{20,28},{24,16},{28,20},{1,9},{5... | collective-permute-start | bytes 786440 | tf_op jit(solution)/shard_map/ppermute | solution.py:14
  197.5 12.9 %collective-permute-start.5 = (f32[2,512,2,32]{1,3,2,0:T(8,128)S(1)}, f32[2,512,2,32]{1,3,2,0:T(8,128)S(1)}, u32[]{:S(2)}, u32[]{:S(2)}) collective-permute-start(f32[2,512,2,32]{1,3,2,0:T(8,128)S(1)} %fusion.20), channel_id=1, source_target_pairs={{0,16},{4,20},{8,24},{12,28},{16,0},{20,4},{24,8},{28,12},{1,17},{... | collective-permute-start | bytes 786440 | tf_op jit(solution)/shard_map/ppermute | solution.py:14
Sparse Core Ops, SparseCore 0:
  10.0 49.5 all-gather.7
  61.1 32.9 all-gather.5
  95.7 34.4 all-gather.3
  216.5 88.3 reduce-scatter.1
where the time goes:
time: 315 us
  waiting for transfers between devices  208 us (66%)
  blocking collectives  34.1 us (11%)
  matrix products  34 us (11%)
  between operations  15.1 us (5%)
  starting transfers between devices  13.8 us (4%)
  other arithmetic  5.63 us (2%)
  local copies, waits for them, and re-layouts  3.65 us (1%)
    reduce_scatter x1, waiting for transfers between devices, local(): lax.psum_scatter(jnp.concatenate([inward, outward], axis=1), 'seq', scatt...  88.5 us
    ppermute x6, waiting for transfers between devices, swapped(): return lax.ppermute(value, axis, pairs)  35.6 us
    all_gather x1, waiting for transfers between devices, local(): lax.all_gather(tokens, 'chan', axis=1, tiled=True)  34.6 us
    all_gather x1, blocking collectives, local(): lax.all_gather(out_weight, 'seq', axis=0, tiled=True)  34.1 us
    all_gather x1, waiting for transfers between devices, local(): lax.all_gather(grad_out, 'chan', axis=1, tiled=True)  31.8 us
    all_gather x1, waiting for transfers between devices, local(): lax.all_gather(in_weight, 'seq', axis=0, tiled=True)  15.8 us
    ppermute x6, starting transfers between devices, swapped(): return lax.ppermute(value, axis, pairs)  13.7 us
    dot_general x2, matrix products, transform(): along_sin = jnp.einsum(formula, sine_table, packed, precision=precise)  10.1 us
  transfers between devices with their start and end apart: 10, of which 10 were waited for; matrix products, arithmetic and copies ran while one was open for 3% of the time, Pallas kernels for 0%

commit v1 on v0

v1 whole, which is shorter than its diff:
```python
import functools
import math

import jax
import jax.numpy as jnp
from jax import lax
from jax.experimental import pallas as pl
from jax.experimental.pallas import tpu as pltpu
from jax.sharding import PartitionSpec as P

precise = lax.Precision.HIGHEST
MESH = pl.DeviceIdType.MESH


def remote(source, target, send_sem, recv_sem, device):
    return pltpu.make_async_remote_copy(
        src_ref=source,
        dst_ref=target,
        send_sem=send_sem,
        recv_sem=recv_sem,
        device_id=device,
        device_id_type=MESH,
    )


def greet(devices_seq, devices_chan, seq_wide):
    seq, chan = lax.axis_index("seq"), lax.axis_index("chan")
    barrier = pltpu.get_barrier_semaphore()
    count = 0
    if seq_wide == "all":

        def hello(step, carry):
            pl.semaphore_signal(
                barrier,
                inc=1,
                device_id=(lax.rem(seq + step, devices_seq), chan),
                device_id_type=MESH,
            )
            return carry

        lax.fori_loop(1, devices_seq, hello, 0)
        count += devices_seq - 1
    else:
        groups = devices_seq // 2

        def hello_group(step, carry):
            there = lax.rem(seq // 2 + step, groups) * 2 + seq % 2
            pl.semaphore_signal(barrier, inc=1, device_id=(there, chan), device_id_type=MESH)
            return carry

        lax.fori_loop(1, groups, hello_group, 0)
        pl.semaphore_signal(
            barrier, inc=1, device_id=(seq + 1 - 2 * (seq % 2), chan), device_id_type=MESH
        )
        count += groups
    if devices_chan:
        groups = devices_chan // 2
        for step in range(1, groups):
            there = lax.rem(chan // 2 + step, groups) * 2 + chan % 2
            pl.semaphore_signal(barrier, inc=1, device_id=(seq, there), device_id_type=MESH)
        pl.semaphore_signal(
            barrier, inc=1, device_id=(seq, chan + 1 - 2 * (chan % 2)), device_id_type=MESH
        )
        count += groups
    pl.semaphore_wait(barrier, count)


def gather_kernel(
    devices_seq,
    devices_chan,
    tokens,
    grads,
    weights,
    all_tokens,
    all_grads,
    all_weights,
    keep_sem,
    chan_send,
    chan_recv,
    chan_pass,
    chan_passed,
    seq_send,
    seq_recv,
    seq_pass,
    seq_passed,
):
    seq, chan = lax.axis_index("seq"), lax.axis_index("chan")
    seq_groups, chan_groups = devices_seq // 2, devices_chan // 2
    seq_pair = (seq + 1 - 2 * (seq % 2), chan)
    chan_pair = (seq, chan + 1 - 2 * (chan % 2))
    columns = tokens.shape[1]
    rows = weights.shape[0]
    greet(devices_seq, devices_chan, "pairs")

    def block(ref, index):
        return ref.at[:, pl.ds(pl.multiple_of(index * columns, columns), columns)]

    def piece(index):
        return all_weights.at[pl.ds(pl.multiple_of(index * rows, rows), rows)]

    def chan_member(step, parity):
        return lax.rem(chan // 2 - step + chan_groups, chan_groups) * 2 + parity

    def seq_member(step, parity):
        return lax.rem(seq // 2 - step + seq_groups, seq_groups) * 2 + parity

    pairs = ((tokens, all_tokens), (grads, all_grads))

    def chan_copy(array, step):
        own, whole = pairs[array]
        there = lax.rem(chan // 2 + step, chan_groups) * 2 + chan % 2
        return remote(
            own,
            block(whole, chan),
            chan_send.at[array, step],
            chan_recv.at[array, step],
            (seq, there),
        )

    def chan_forward(array, step):
        own, whole = pairs[array]
        here = chan_member(step, chan % 2)
        return remote(
            own if step == 0 else block(whole, here),
            block(whole, here),
            chan_pass.at[array, step],
            chan_passed.at[array, step],
            chan_pair,
        )

    def seq_copy(step):
        there = lax.rem(seq // 2 + step, seq_groups) * 2 + seq % 2
        return remote(weights, piece(seq), seq_send.at[step], seq_recv.at[step], (there, chan))

    def seq_forward(step):
        here = seq_member(step, seq % 2)
        return remote(piece(here), piece(here), seq_pass.at[step], seq_passed.at[step], seq_pair)

    own_piece = remote(weights, piece(seq), seq_pass.at[0], seq_passed.at[0], seq_pair)

    def each(call):
        def body(step, carry):
            call(step)
            return carry

        lax.fori_loop(1, seq_groups, body, 0)

    for array in range(2):
        for step in range(1, chan_groups):
            chan_copy(array, step).start()
    each(lambda step: seq_copy(step).start())
    own_piece.start()
    for array in range(2):
        chan_forward(array, 0).start()
    keeps = [
        pltpu.make_async_copy(tokens, block(all_tokens, chan), keep_sem.at[0]),
        pltpu.make_async_copy(grads, block(all_grads, chan), keep_sem.at[1]),
        pltpu.make_async_copy(weights, piece(seq), keep_sem.at[2]),
    ]
    for keep in keeps:
        keep.start()

    def pass_on(step):
        seq_copy(step).wait_recv()
        seq_forward(step).start()

    each(pass_on)
    for array in range(2):
        for step in range(1, chan_groups):
            chan_copy(array, step).wait_recv()
            chan_forward(array, step).start()
    for keep in keeps:
        keep.wait()
    own_piece.wait()

    def finish(step):
        seq_copy(step).wait_send()
        seq_forward(step).wait()

    each(finish)
    for array in range(2):
        for step in range(chan_groups):
            chan_forward(array, step).wait()
        for step in range(1, chan_groups):
            chan_copy(array, step).wait_send()


def gathered(tokens, grads, weights):
    devices_seq, devices_chan = lax.axis_size("seq"), lax.axis_size("chan")
    dma = pltpu.SemaphoreType.DMA
    seq_groups, chan_groups = devices_seq // 2, devices_chan // 2
    vmem, anywhere = pl.BlockSpec(memory_space=pltpu.VMEM), pl.BlockSpec(memory_space=pl.ANY)
    wide = jax.ShapeDtypeStruct((tokens.shape[0], tokens.shape[1] * devices_chan), tokens.dtype)
    tall = jax.ShapeDtypeStruct((weights.shape[0] * devices_seq, weights.shape[1]), weights.dtype)
    return pl.pallas_call(
        functools.partial(gather_kernel, devices_seq, devices_chan),
        out_shape=(wide, wide, tall),
        in_specs=[vmem] * 3,
        out_specs=(anywhere,) * 3,
        scratch_shapes=[dma((3,))]
        + [dma((2, chan_groups))] * 4
        + [dma((seq_groups,))] * 4,
        compiler_params=pltpu.CompilerParams(collective_id=0, has_side_effects=True),
        name="gather_inputs",
    )(tokens, grads, weights)


def states_kernel(devices_seq, own, whole, send, recv):
    seq, chan = lax.axis_index("seq"), lax.axis_index("chan")
    greet(devices_seq, 0, "all")

    def copy(step):
        there = lax.rem(seq + step, devices_seq)
        return remote(own, whole.at[seq], send.at[step], recv.at[step], (there, chan))

    def start(step, carry):
        copy(step).start()
        return carry

    def wait(step, carry):
        copy(step).wait()
        return carry

    lax.fori_loop(1, devices_seq, start, 0)
    whole[seq] = own[...]
    lax.fori_loop(1, devices_seq, wait, 0)


def gathered_states(state):
    devices_seq = lax.axis_size("seq")
    vmem = pl.BlockSpec(memory_space=pltpu.VMEM)
    return pl.pallas_call(
        functools.partial(states_kernel, devices_seq),
        out_shape=jax.ShapeDtypeStruct((devices_seq,) + state.shape, state.dtype),
        in_specs=[vmem],
        out_specs=vmem,
        scratch_shapes=[pltpu.SemaphoreType.DMA((devices_seq,))] * 2,
        compiler_params=pltpu.CompilerParams(collective_id=1, has_side_effects=True),
        name="gather_states",
    )(state)


def reduce_kernel(
    devices_seq, parts, total, near, paired, far, pair_send, pair_recv, far_send, far_recv
):
    seq, chan = lax.axis_index("seq"), lax.axis_index("chan")
    groups = devices_seq // 2
    group, parity = seq // 2, seq % 2
    greet(devices_seq, 0, "pairs")

    def member(step):
        return lax.rem(group + step, groups)

    def pair_copy(step):
        return remote(
            parts.at[member(step) * 2 + 1 - parity],
            near.at[step],
            pair_send.at[step],
            pair_recv.at[step],
            (group * 2 + 1 - parity, chan),
        )

    def far_copy(step):
        return remote(
            paired.at[step],
            far.at[step],
            far_send.at[step],
            far_recv.at[step],
            (member(step) * 2 + parity, chan),
        )

    def each(call):
        def body(step, carry):
            call(step)
            return carry

        lax.fori_loop(1, groups, body, 0)

    def pair_sum(step):
        own = parts[member(step) * 2 + parity].astype(jnp.float32)
        return own + near[step].astype(jnp.float32)

    each(lambda step: pair_copy(step).start())
    pair_copy(0).start()

    def pass_on(step):
        pair_copy(step).wait_recv()
        paired[step] = pair_sum(step).astype(paired.dtype)
        far_copy(step).start()

    each(pass_on)
    pair_copy(0).wait_recv()
    total[...] = pair_sum(0)

    def collect(step):
        far_copy(step).wait_recv()
        total[...] += far[step].astype(jnp.float32)

    each(collect)

    def finish(step):
        pair_copy(step).wait_send()
        far_copy(step).wait_send()

    each(finish)
    pair_copy(0).wait_send()


def reduced(parts):
    devices_seq = lax.axis_size("seq")
    groups = devices_seq // 2
    shape = parts.shape[1:]
    vmem = pl.BlockSpec(memory_space=pltpu.VMEM)
    return pl.pallas_call(
        functools.partial(reduce_kernel, devices_seq),
        out_shape=jax.ShapeDtypeStruct(shape, jnp.float32),
        in_specs=[vmem],
        out_specs=vmem,
        scratch_shapes=[pltpu.VMEM((groups,) + shape, parts.dtype)] * 3
        + [pltpu.SemaphoreType.DMA((groups,))] * 4,
        compiler_params=pltpu.CompilerParams(collective_id=2, has_side_effects=True),
        name="reduce_owned",
    )(parts)


def correlate(signal, residues, decay_length):
    rows, channels = signal.shape
    devices_seq = lax.axis_size("seq")
    position = lax.axis_index("seq")
    chunk = min(64, rows)
    chunks = rows // chunk
    per_filter = channels // residues.shape[1]
    rate = jnp.repeat(1.0 / decay_length, per_filter, axis=1)
    weight = jnp.repeat(residues, per_filter, axis=1) * jnp.sqrt(-jnp.expm1(-2.0 * rate))
    offset = jnp.arange(chunk, dtype=jnp.float32)
    exponent = rate.T[:, :, None] * offset
    grow = weight.T[:, :, None] * jnp.exp(exponent)
    fall = jnp.exp(-exponent)
    later = jnp.arange(chunk)[None, :] >= jnp.arange(chunk)[:, None]
    taps = jnp.einsum("cri,crj->cij", grow, fall, precision=precise)
    taps = jnp.where(later, taps, 0.0)
    pieces = signal.reshape(chunks, chunk, channels).transpose(2, 1, 0)
    both = jnp.einsum(
        "cij,cjn->cin", jnp.concatenate([taps, fall], axis=1), pieces, precision=precise
    )
    inner, sums = both[:, :chunk], both[:, chunk:]
    step = jnp.exp(-chunk * rate).T
    state = jnp.zeros_like(step)
    entering = []
    for index in reversed(range(chunks)):
        entering.append(step * state)
        state = sums[:, :, index] + step * state
    entering = jnp.stack(entering[::-1], axis=2)
    states = gathered_states(state)
    gap = (jnp.arange(devices_seq) - position - 1).astype(jnp.float32) * rows
    scale = jnp.where(
        gap[:, None, None] >= 0.0,
        jnp.exp(-jnp.maximum(gap, 0.0)[:, None, None] * rate.T),
        0.0,
    )
    following = jnp.sum(scale * states, axis=0)
    reach = (chunks - jnp.arange(chunks)).astype(jnp.float32) * chunk
    entering = entering + following[:, :, None] * jnp.exp(-rate.T[:, :, None] * reach)
    outer = jnp.einsum("cri,crn->cin", grow, entering, precision=precise)
    return (inner + outer).transpose(2, 1, 0).reshape(rows, channels)


def local(tokens, grad_out, in_weight, out_weight, conv_out, residues, decay_length):
    local_rows = tokens.shape[0]
    channels = out_weight.shape[1]
    owned_rows = in_weight.shape[0]
    weights = jnp.concatenate([in_weight.reshape(owned_rows, 3 * channels), out_weight], axis=1)
    full_tokens, full_grads, full_weights = gathered(tokens, grad_out, weights)
    projected = jnp.dot(
        full_tokens, full_weights[:, : 3 * channels], preferred_element_type=jnp.float32
    )
    upstream = jnp.dot(
        full_grads, full_weights[:, 3 * channels :], preferred_element_type=jnp.float32
    )
    streams = projected.astype(jnp.bfloat16).astype(jnp.float32)
    gate_first = streams[:, :channels]
    gate_second = streams[:, channels : 2 * channels]
    value_stream = streams[:, 2 * channels :]
    conv_value = conv_out.astype(jnp.float32)
    gated = (gate_second * conv_value).astype(jnp.bfloat16)
    grad_second = (upstream * conv_value).astype(jnp.bfloat16)
    grad_conv = upstream * gate_second
    grad_source = correlate(grad_conv, residues, decay_length)
    grad_first = (grad_source * value_stream).astype(jnp.bfloat16)
    grad_value = (grad_source * gate_first).astype(jnp.bfloat16)
    grad_streams = jnp.concatenate([grad_first, grad_second, grad_value], axis=1)
    inward = lax.dot_general(
        full_tokens, grad_streams, (((0,), (0,)), ((), ())), preferred_element_type=jnp.float32
    )
    outward = lax.dot_general(
        full_grads, gated, (((0,), (0,)), ((), ())), preferred_element_type=jnp.float32
    )
    parts = jnp.concatenate([inward, outward], axis=1).astype(jnp.bfloat16)
    owned = reduced(parts.reshape(-1, owned_rows, 4 * channels))
    grad_in = owned[:, : 3 * channels].reshape(owned_rows, 3, channels)
    grad_proj = owned[:, 3 * channels :]
    return (grad_in, grad_proj)


def solution(mesh):
    return jax.shard_map(
        local,
        mesh=mesh,
        in_specs=(
            P("seq", "chan"),
            P("seq", "chan"),
            P("seq", None, "chan"),
            P("seq", "chan"),
            P("seq", "chan"),
            P(None, "chan"),
            P(None, "chan"),
        ),
        out_specs=(P("seq", None, "chan"), P("seq", "chan")),
        check_vma=False,
    )
```

time: 315 us -> 146 us (0.46)
  waiting for transfers between devices: 208 us -> 0 us
  Pallas kernels: 0 us -> 102 us
  blocking collectives: 34.1 us -> 0 us
  between operations: 15.1 us -> 0.89 us
  starting transfers between devices: 13.8 us -> 0 us
  matrix products: 34 us -> 24.3 us
  local copies, waits for them, and re-layouts: 3.65 us -> 13.2 us
    pallas_call x0 -> x3, Pallas kernels: none -> 102 us  [the longest x1 56.5 us: gathered(): pl.pallas_call(functools.partial(gather_kernel, devices_seq, devices_chan...]
    reduce_scatter x1 -> x0, waiting for transfers between devices: 88.5 us -> none  [local(): lax.psum_scatter(jnp.concatenate([inward, outward], axis=1), 'seq', scatt...]
    all_gather x3 -> x0, waiting for transfers between devices: 82.2 us -> none  [the longest x1 34.6 us: local(): lax.all_gather(tokens, 'chan', axis=1, tiled=True)]
    ppermute x6 -> x0, waiting for transfers between devices: 35.6 us -> none  [swapped(): return lax.ppermute(value, axis, pairs)]
    all_gather x1 -> x0, blocking collectives: 34.1 us -> none  [local(): lax.all_gather(out_weight, 'seq', axis=0, tiled=True)]
    ppermute x6 -> x0, starting transfers between devices: 13.7 us -> none  [swapped(): return lax.ppermute(value, axis, pairs)]
    dot_general x8 -> x7, matrix products: 34 us -> 24.3 us  [the longest x1 5.25 us: correlate(): taps = jnp.einsum('cri,crj->cij', grow, fall, precision=precise)]
    another operation x0 -> x11, local copies, waits for them, and re-layouts: none -> 5.32 us
  transfers between devices with their start and end apart: 10 -> 0, of which waited for: 10 -> 0; matrix products, arithmetic and copies ran while one was open for 3% -> 0% of each run, Pallas kernels for 0% -> 0%
where the time goes in v1:
time: 146 us; the launch traced here: 145 us
  Pallas kernels  102 us (70%)
  matrix products  24.3 us (17%)
  local copies, waits for them, and re-layouts  13.2 us (9%)
  other arithmetic  4.98 us (3%)
    pallas_call x1, Pallas kernels, gathered(): pl.pallas_call(functools.partial(gather_kernel, devices_seq, devices_chan...  56.5 us
    pallas_call x1, Pallas kernels, reduced(): pl.pallas_call(functools.partial(reduce_kernel, devices_seq), out_shape=j...  34.9 us
    pallas_call x1, Pallas kernels, gathered_states(): pl.pallas_call(functools.partial(states_kernel, devices_seq), out_shape=j...  10.3 us
    dot_general x1, matrix products, correlate(): taps = jnp.einsum('cri,crj->cij', grow, fall, precision=precise)  5.25 us
    another operation x2, local copies, waits for them, and re-layouts  4.66 us
    dot_general x1, matrix products, local(): jnp.dot(full_tokens, full_weights[:, :3 * channels], preferred_element_ty...  4.53 us
    dot_general x1, matrix products, local(): lax.dot_general(full_tokens, grad_streams, (((0,), (0,)), ((), ())), pref...  4.39 us
    dot_general x1, matrix products, local(): lax.dot_general(full_grads, gated, (((0,), (0,)), ((), ())), preferred_el...  3.85 us

profile of v1, /device:TPU:0, one launch (start us, length us, event | category | flops | bytes accessed | tf_op | source)
XLA Modules:
  0.0 145.2 jit_solution(13185607525485311126)
XLA Ops:
  0.6 1.1 copy.104
  1.7 1.0 copy.105
  2.7 0.8 pad_maximum_fusion.1.weights
  3.5 56.5 %gather_inputs.1 = (bf16[512,4096]{1,0:T(8,128)(2,1)}, bf16[512,4096]{1,0:T(8,128)(2,1)}, bf16[4096,256]{1,0:T(8,128)(2,1)}) custom-call(bf16[512,1024]{1,0:T(8,128)(2,1)} %tokens.1, bf16[512,1024]{1,0:T(8,128)(2,1)} %grads.1, bf16[512,256]{1,0:T(8,128)(2,1)} %pad_maximum_fusion.1.weights), custom_call_target="tpu_custom_call" | custom-call | tf_op jit(solution)/shard_map/gather_inputs/pallas_call | solution.py:195
  60.0 0.0 copy-start
  60.0 0.0 copy-start.1
  60.1 0.0 copy-start.2
  60.1 4.5 %fusion.9 = f32[512,192]{0,1:T(8,128)S(1)} fusion(bf16[512,4096]{1,0:T(8,128)(2,1)} %get-tuple-element.5, bf16[4096,256]{1,0:T(8,128)(2,1)} %get-tuple-element.7), kind=kOutput, calls=%fused_computation.11 | convolution fusion | flops 805502976 | bytes 6684672 | tf_op jit(solution)/shard_map/dot_general | solution.py:374
  64.6 0.0 copy-done
  64.6 0.2 copy-done.1
  64.8 0.0 copy-done.2
  64.8 1.7 %fusion.25 = (bf16[512,64]{0,1:T(8,128)(2,1)S(1)}, f32[512,64]{0,1:T(8,128)S(1)}) fusion(bf16[512,64]{0,1:T(8,128)(2,1)S(1)} %copy-done.2, f32[512,192]{0,1:T(8,128)S(1)} %fusion.9, bf16[512,4096]{1,0:T(8,128)(2,1)S(1)} %copy-done, bf16[4096,256]{1,0:T(8,128)(2,1)S(1)} %copy-done.1), kind=kOutput, calls=%fused_computation.33 | convolution fusion | flops 268566528 | bytes 5636096 | tf_op jit(solution)/shard_map/dot_general | solution.py:377
  66.5 0.1 reshape.56
  66.6 0.1 copy.107
  66.7 0.0 copy-done.3
  66.7 0.1 copy.106
  66.9 5.2 %convolution_select_fusion = f32[64,64,64]{1,2,0:T(8,128)} fusion(pred[64,64]{0,1:T(8,128)(4,1)S(1)} %iota_compare_fusion, f32[64,16]{1,0:T(8,128)S(1)} %bitcast.104, f32[64,16]{1,0:T(8,128)S(1)} %multiply_bitcast_fusion), kind=kOutput, calls=%fused_computation.9 | convolution fusion | flops 50855936 | bytes 1060864 | tf_op jit(solution)/shard_map/cri,crj->cij/dot_general | solution.py:340
  72.1 0.2 negate_exponential_fusion
  72.4 0.6 copy.108
  73.0 3.8 %fusion = f32[64,80,8]{1,2,0:T(8,128)S(1)} fusion(f32[64,16,64]{1,2,0:T(8,128)S(1)} %copy.108, f32[64,64,64]{1,2,0:T(8,128)} %convolution_select_fusion, f32[8,64,64]{1,0,2:T(8,128)S(1)} %reshape.56), kind=kOutput, calls=%fused_computation.2 | convolution fusion | flops 31784960 | bytes 1605632 | tf_op jit(solution)/shard_map/cij,cjn->cin/dot_general | solution.py:343
  76.8 0.6 fusion.39
  77.4 0.7 fusion.38
  78.0 10.3 %gather_states.1 = f32[8,64,16]{2,1,0:T(8,128)} custom-call(f32[64,16]{1,0:T(8,128)} %get-tuple-element.18.own), custom_call_target="tpu_custom_call" | custom-call | tf_op jit(solution)/shard_map/gather_states/pallas_call | solution.py:232
  88.4 1.1 multiply_reduce_fusion
  89.5 0.1 copy.125
  89.6 0.1 copy.117
  89.6 0.1 copy.118
  89.7 0.1 copy.123
  89.8 0.1 copy.116
  89.8 0.1 copy.119
  89.9 0.1 copy.120
  89.9 0.1 copy.121
  90.0 0.1 copy.122
  90.1 0.2 stack.35
  90.3 0.1 copy.126
  90.3 0.1 multiply_add_fusion
  90.4 0.2 copy.127
  90.6 0.8 fusion.12
  91.4 0.1 reshape.57
  91.6 4.4 %convolution_convert_fusion = bf16[4096,192]{0,1:T(8,128)(2,1)} fusion(bf16[512,4096]{1,0:T(8,128)(2,1)} %get-tuple-element.5, bf16[512,64]{0,1:T(8,128)(2,1)S(1)} %get-tuple-element.22, bf16[512,64]{0,1:T(8,128)(2,1)S(1)} %get-tuple-element.31, bf16[512,64]{0,1:T(8,128)(2,1)S(1)} %get-tuple-element.21), kind=kOutput, calls=%fused_computation | convolution fusion | flops 806682624 | bytes 5963776 | tf_op jit(solution)/shard_map/dot_general | solution.py:392
  95.9 3.1 %copy.128 = bf16[4096,192]{1,0:T(8,128)(2,1)S(1)} copy(bf16[4096,192]{0,1:T(8,128)(2,1)} %convolution_convert_fusion) | data formatting | bytes 3145728 | tf_op jit(solution)/shard_map/convert.3
  99.1 3.8 %convolution_convert_fusion.1 = bf16[4096,64]{0,1:T(8,128)(2,1)} fusion(bf16[512,4096]{1,0:T(8,128)(2,1)} %get-tuple-element.6, bf16[512,64]{0,1:T(8,128)(2,1)S(1)} %copy-done.2, f32[512,192]{0,1:T(8,128)S(1)} %fusion.9), kind=kOutput, calls=%fused_computation.1 | convolution fusion | flops 268795904 | bytes 4915200 | tf_op jit(solution)/shard_map/dot_general | solution.py:395
  103.0 1.5 %copy.129 = bf16[4096,64]{1,0:T(8,128)(2,1)S(1)} copy(bf16[4096,64]{0,1:T(8,128)(2,1)} %convolution_convert_fusion.1) | data formatting | bytes 1048576 | tf_op jit(solution)/shard_map/convert.2
  104.5 2.0 %pad_maximum_fusion.parts = bf16[8,512,256]{2,1,0:T(8,128)(2,1)} fusion(bf16[8,512,64]{2,1,0:T(8,128)(2,1)S(1)} %bitcast.101, bf16[8,512,192]{2,1,0:T(8,128)(2,1)S(1)} %bitcast.100), kind=kLoop, calls=%fused_computation.6 | loop fusion | flops 4194304 | bytes 4194304 | tf_op jit(solution)/shard_map/concatenate | solution.py:398
  106.5 34.9 %reduce_owned.1 = f32[512,256]{1,0:T(8,128)} custom-call(bf16[8,512,256]{2,1,0:T(8,128)(2,1)} %pad_maximum_fusion.parts), custom_call_target="tpu_custom_call" | custom-call | tf_op jit(solution)/shard_map/reduce_owned/pallas_call | solution.py:314
  141.4 2.0 %copy.130 = f32[512,192]{0,1:T(8,128)} copy(f32[512,192]{1,0:T(8,128)} %bitcast.102) | data formatting | bytes 786432 | tf_op jit(solution)/shard_map/slice | solution.py:400
  143.3 1.1 slice.72
  144.4 0.8 copy.131
  (14 shorter events, 0.2 us)
Async XLA Ops:
  60.0 4.6 %copy-start = (bf16[512,4096]{1,0:T(8,128)(2,1)S(1)}, bf16[512,4096]{1,0:T(8,128)(2,1)}, u32[]{:S(2)}) copy-start(bf16[512,4096]{1,0:T(8,128)(2,1)} %get-tuple-element.6) | copy-start | bytes 12582916
  60.0 4.7 %copy-start.1 = (bf16[4096,256]{1,0:T(8,128)(2,1)S(1)}, bf16[4096,256]{1,0:T(8,128)(2,1)}, u32[]{:S(2)}) copy-start(bf16[4096,256]{1,0:T(8,128)(2,1)} %get-tuple-element.7) | copy-start | bytes 6291460
  60.1 4.7 %copy-start.2 = (bf16[512,64]{0,1:T(8,128)(2,1)S(1)}, bf16[512,64]{0,1:T(8,128)(2,1)}, u32[]{:S(2)}) copy-start(bf16[512,64]{0,1:T(8,128)(2,1)} %param.11) | copy-start | bytes 196612
  64.8 1.9 %copy-start.4 = (f32[16,32]{1,0:T(8,128)S(1)}, f32[16,32]{1,0:T(8,128)}, u32[]{:S(2)}) copy-start(f32[16,32]{1,0:T(8,128)} %param.13) | copy-start | bytes 6148
  64.8 2.0 %copy-start.3 = (f32[16,32]{1,0:T(8,128)S(1)}, f32[16,32]{1,0:T(8,128)}, u32[]{:S(2)}) copy-start(f32[16,32]{1,0:T(8,128)} %param.12) | copy-start | bytes 6148

commit v2 on v1

--- a/solution.py
+++ b/solution.py
@@ -205,128 +205,196 @@
     )(tokens, grads, weights)
 
 
-def states_kernel(devices_seq, own, whole, send, recv):
-    seq, chan = lax.axis_index("seq"), lax.axis_index("chan")
-    greet(devices_seq, 0, "all")
-
-    def copy(step):
-        there = lax.rem(seq + step, devices_seq)
-        return remote(own, whole.at[seq], send.at[step], recv.at[step], (there, chan))
-
-    def start(step, carry):
-        copy(step).start()
-        return carry
-
-    def wait(step, carry):
-        copy(step).wait()
-        return carry
-
-    lax.fori_loop(1, devices_seq, start, 0)
-    whole[seq] = own[...]
-    lax.fori_loop(1, devices_seq, wait, 0)
-
-
-def gathered_states(state):
-    devices_seq = lax.axis_size("seq")
-    vmem = pl.BlockSpec(memory_space=pltpu.VMEM)
-    return pl.pallas_call(
-        functools.partial(states_kernel, devices_seq),
-        out_shape=jax.ShapeDtypeStruct((devices_seq,) + state.shape, state.dtype),
-        in_specs=[vmem],
-        out_specs=vmem,
-        scratch_shapes=[pltpu.SemaphoreType.DMA((devices_seq,))] * 2,
-        compiler_params=pltpu.CompilerParams(collective_id=1, has_side_effects=True),
-        name="gather_states",
-    )(state)
-
-
 def reduce_kernel(
-    devices_seq, parts, total, near, paired, far, pair_send, pair_recv, far_send, far_recv
+    devices_seq,
+    tile,
+    state,
+    rate,
+    weight,
+    inner,
+    value,
+    gate,
+    early_in,
+    early_out,
+    tokens_hbm,
+    grads_hbm,
+    total,
+    tokens,
+    grads,
+    states,
+    late,
+    parts,
+    near,
+    paired,
+    far,
+    load_sem,
+    state_send,
+    state_recv,
+    pair_send,
+    pair_recv,
+    far_send,
+    far_recv,
 ):
     seq, chan = lax.axis_index("seq"), lax.axis_index("chan")
     groups = devices_seq // 2
     group, parity = seq // 2, seq % 2
-    greet(devices_seq, 0, "pairs")
-
-    def member(step):
-        return lax.rem(group + step, groups)
-
-    def pair_copy(step):
-        return remote(
-            parts.at[member(step) * 2 + 1 - parity],
-            near.at[step],
-            pair_send.at[step],
-            pair_recv.at[step],
-            (group * 2 + 1 - parity, chan),
-        )
-
-    def far_copy(step):
-        return remote(
-            paired.at[step],
-            far.at[step],
-            far_send.at[step],
-            far_recv.at[step],
-            (member(step) * 2 + parity, chan),
-        )
-
-    def each(call):
+    rows, channels = inner.shape
+    owned = near.shape[2]
+    loads = [
+        pltpu.make_async_copy(tokens_hbm, tokens, load_sem.at[0]),
+        pltpu.make_async_copy(grads_hbm, grads, load_sem.at[1]),
+    ]
+    for load in loads:
+        load.start()
+    greet(devices_seq, 0, "all")
+
+    def loop(start, stop, call):
         def body(step, carry):
             call(step)
             return carry
 
-        lax.fori_loop(1, groups, body, 0)
-
-    def pair_sum(step):
-        own = parts[member(step) * 2 + parity].astype(jnp.float32)
-        return own + near[step].astype(jnp.float32)
-
-    each(lambda step: pair_copy(step).start())
-    pair_copy(0).start()
-
-    def pass_on(step):
-        pair_copy(step).wait_recv()
-        paired[step] = pair_sum(step).astype(paired.dtype)
-        far_copy(step).start()
-
-    each(pass_on)
-    pair_copy(0).wait_recv()
-    total[...] = pair_sum(0)
-
-    def collect(step):
-        far_copy(step).wait_recv()
-        total[...] += far[step].astype(jnp.float32)
-
-    each(collect)
-
-    def finish(step):
-        pair_copy(step).wait_send()
-        far_copy(step).wait_send()
-
-    each(finish)
-    pair_copy(0).wait_send()
-
-
-def reduced(parts):
+        lax.fori_loop(start, stop, body, 0)
+
+    def state_copy(step):
+        there = lax.rem(seq + step, devices_seq)
+        return remote(
+            state, states.at[step], state_send.at[step], state_recv.at[step], (there, chan)
+        )
+
+    def member(step):
+        return lax.rem(group + step, groups)
+
+    def piece(half, index):
+        return parts.at[half, pl.ds(pl.multiple_of(index * owned, owned), owned)]
+
+    def pair_copy(half, step):
+        return remote(
+            piece(half, member(step) * 2 + 1 - parity),
+            near.at[half, step],
+            pair_send.at[half, step],
+            pair_recv.at[half, step],
+            (group * 2 + 1 - parity, chan),
+        )
+
+    def far_copy(half, step):
+        return remote(
+            paired.at[half, step],
+            far.at[half, step],
+            far_send.at[half, step],
+            far_recv.at[half, step],
+            (member(step) * 2 + parity, chan),
+        )
+
+    def summed(left, right):
+        return lax.dot_general(
+            left, right, (((0,), (0,)), ((), ())), preferred_element_type=jnp.float32
+        )
+
+    def span(index):
+        return pl.ds(pl.multiple_of(index * tile, tile), tile)
+
+    loop(1, devices_seq, lambda step: state_copy(step).start())
+    for load in loads:
+        load.wait()
+
+    def early_tile(index):
+        product = summed(tokens[:, span(index)], early_in[...])
+        product += summed(grads[:, span(index)], early_out[...])
+        parts[0, span(index)] = product.astype(parts.dtype)
+
+    loop(0, tokens.shape[1] // tile, early_tile)
+    loop(1, groups, lambda step: pair_copy(0, step).start())
+    pair_copy(0, 0).start()
+
+    def absorb(step, following):
+        state_copy(step).wait_recv()
+        gap = lax.rem(seq - step + devices_seq, devices_seq) - seq - 1
+        reach = (jnp.maximum(gap, 0) * rows).astype(jnp.float32)
+        present = (gap >= 0).astype(jnp.float32)
+        return following + present * states[step] * jnp.exp(-reach * rate[...])
+
+    following = lax.fori_loop(1, devices_seq, absorb, jnp.zeros(rate.shape, jnp.float32))
+    entering = weight[...] * following
+    rates = rate[...]
+    band = math.gcd(rows, 64)
+
+    def source_rows(index):
+        here = pl.ds(pl.multiple_of(index * band, band), band)
+        position = lax.broadcasted_iota(jnp.int32, (band, channels), 0) + index * band
+        reach = (rows - position).astype(jnp.float32)
+        source = inner[here]
+        for mode in range(rates.shape[0]):
+            source += entering[mode : mode + 1] * jnp.exp(-reach * rates[mode : mode + 1])
+        late[here] = jnp.concatenate([source * value[here], source * gate[here]], axis=1).astype(
+            late.dtype
+        )
+
+    loop(0, rows // band, source_rows)
+
+    def late_tile(index):
+        parts[1, span(index)] = summed(tokens[:, span(index)], late[...]).astype(parts.dtype)
+
+    loop(0, tokens.shape[1] // tile, late_tile)
+    loop(1, groups, lambda step: pair_copy(1, step).start())
+    pair_copy(1, 0).start()
+
+    def pair_sum(half, step):
+        own = piece(half, member(step) * 2 + parity)[...].astype(jnp.float32)
+        return own + near[half, step].astype(jnp.float32)
+
+    for half in range(2):
+
+        def pass_on(step):
+            pair_copy(half, step).wait_recv()
+            paired[half, step] = pair_sum(half, step).astype(paired.dtype)
+            far_copy(half, step).start()
+
+        loop(1, groups, pass_on)
+    for half in range(2):
+        pair_copy(half, 0).wait_recv()
+        total[half] = pair_sum(half, 0)
+
+        def collect(step):
+            far_copy(half, step).wait_recv()
+            total[half] += far[half, step].astype(jnp.float32)
+
+        loop(1, groups, collect)
+
+        def finish(step):
+            pair_copy(half, step).wait_send()
+            far_copy(half, step).wait_send()
+
+        loop(1, groups, finish)
+        pair_copy(half, 0).wait_send()
+    loop(1, devices_seq, lambda step: state_copy(step).wait_send())
+
+
+def reduced(state, rate, weight, inner, value, gate, early_in, early_out, tokens, grads, owned):
     devices_seq = lax.axis_size("seq")
     groups = devices_seq // 2
-    shape = parts.shape[1:]
-    vmem = pl.BlockSpec(memory_space=pltpu.VMEM)
+    rows, channels = inner.shape
+    width = tokens.shape[1]
+    wide = 2 * channels
+    vmem, anywhere = pl.BlockSpec(memory_space=pltpu.VMEM), pl.BlockSpec(memory_space=pl.ANY)
+    dma, half_type = pltpu.SemaphoreType.DMA, tokens.dtype
     return pl.pallas_call(
-        functools.partial(reduce_kernel, devices_seq),
-        out_shape=jax.ShapeDtypeStruct(shape, jnp.float32),
-        in_specs=[vmem],
+        functools.partial(reduce_kernel, devices_seq, math.gcd(width, 512)),
+        out_shape=jax.ShapeDtypeStruct((2, owned, wide), jnp.float32),
+        in_specs=[vmem] * 8 + [anywhere] * 2,
         out_specs=vmem,
-        scratch_shapes=[pltpu.VMEM((groups,) + shape, parts.dtype)] * 3
-        + [pltpu.SemaphoreType.DMA((groups,))] * 4,
-        compiler_params=pltpu.CompilerParams(collective_id=2, has_side_effects=True),
+        scratch_shapes=[pltpu.VMEM(tokens.shape, half_type)] * 2
+        + [pltpu.VMEM((devices_seq,) + state.shape, jnp.float32)]
+        + [pltpu.VMEM((rows, wide), half_type), pltpu.VMEM((2, width, wide), half_type)]
+        + [pltpu.VMEM((2, groups, owned, wide), half_type)] * 3
+        + [dma((2,)), dma((devices_seq,)), dma((devices_seq,))]
+        + [dma((2, groups))] * 4,
+        compiler_params=pltpu.CompilerParams(collective_id=1, has_side_effects=True),
         name="reduce_owned",
-    )(parts)
-
-
-def correlate(signal, residues, decay_length):
+    )(state, rate, weight, inner, value, gate, early_in, early_out, tokens, grads)
+
+
+def correlate_block(signal, residues, decay_length):
     rows, channels = signal.shape
-    devices_seq = lax.axis_size("seq")
-    position = lax.axis_index("seq")
     chunk = min(64, rows)
     chunks = rows // chunk
     per_filter = channels // residues.shape[1]
@@ -351,18 +419,8 @@
         entering.append(step * state)
         state = sums[:, :, index] + step * state
     entering = jnp.stack(entering[::-1], axis=2)
-    states = gathered_states(state)
-    gap = (jnp.arange(devices_seq) - position - 1).astype(jnp.float32) * rows
-    scale = jnp.where(
-        gap[:, None, None] >= 0.0,
-        jnp.exp(-jnp.maximum(gap, 0.0)[:, None, None] * rate.T),
-        0.0,
-    )
-    following = jnp.sum(scale * states, axis=0)
-    reach = (chunks - jnp.arange(chunks)).astype(jnp.float32) * chunk
-    entering = entering + following[:, :, None] * jnp.exp(-rate.T[:, :, None] * reach)
     outer = jnp.einsum("cri,crn->cin", grow, entering, precision=precise)
-    return (inner + outer).transpose(2, 1, 0).reshape(rows, channels)
+    return (inner + outer).transpose(2, 1, 0).reshape(rows, channels), state.T, rate, weight
 
 
 def local(tokens, grad_out, in_weight, out_weight, conv_out, residues, decay_length):
@@ -377,7 +435,7 @@
     upstream = jnp.dot(
         full_grads, full_weights[:, 3 * channels :], preferred_element_type=jnp.float32
     )
-    streams = projected.astype(jnp.bfloat16).astype(jnp.float32)
+    streams = lax.reduce_precision(projected, exponent_bits=8, mantissa_bits=7)
     gate_first = streams[:, :channels]
     gate_second = streams[:, channels : 2 * channels]
     value_stream = streams[:, 2 * channels :]
@@ -385,21 +443,25 @@
     gated = (gate_second * conv_value).astype(jnp.bfloat16)
     grad_second = (upstream * conv_value).astype(jnp.bfloat16)
     grad_conv = upstream * gate_second
-    grad_source = correlate(grad_conv, residues, decay_length)
-    grad_first = (grad_source * value_stream).astype(jnp.bfloat16)
-    grad_value = (grad_source * gate_first).astype(jnp.bfloat16)
-    grad_streams = jnp.concatenate([grad_first, grad_second, grad_value], axis=1)
-    inward = lax.dot_general(
-        full_tokens, grad_streams, (((0,), (0,)), ((), ())), preferred_element_type=jnp.float32
-    )
-    outward = lax.dot_general(
-        full_grads, gated, (((0,), (0,)), ((), ())), preferred_element_type=jnp.float32
-    )
-    parts = jnp.concatenate([inward, outward], axis=1).astype(jnp.bfloat16)
-    owned = reduced(parts.reshape(-1, owned_rows, 4 * channels))
-    grad_in = owned[:, : 3 * channels].reshape(owned_rows, 3, channels)
-    grad_proj = owned[:, 3 * channels :]
-    return (grad_in, grad_proj)
+    inner, state, rate, weight = correlate_block(grad_conv, residues, decay_length)
+    blank = jnp.zeros_like(gated)
+    owned = reduced(
+        state,
+        rate,
+        weight,
+        inner,
+        value_stream,
+        gate_first,
+        jnp.concatenate([grad_second, blank], axis=1),
+        jnp.concatenate([blank, gated], axis=1),
+        full_tokens,
+        full_grads,
+        owned_rows,
+    )
+    grad_in = jnp.stack(
+        [owned[1, :, :channels], owned[0, :, :channels], owned[1, :, channels:]], axis=1
+    )
+    return (grad_in, owned[0, :, channels:])
 
 
 def solution(mesh):

time: 146 us -> 127 us (0.87)
  Pallas kernels: 102 us -> 95.9 us
  matrix products: 24.3 us -> 18.4 us
  local copies, waits for them, and re-layouts: 13.2 us -> 9.4 us
  other arithmetic: 4.98 us -> 1.97 us
    dot_general x5 -> x3, matrix products: 18.1 us -> 9.9 us  [the longest x1 3.94 us: correlate_block(): taps = jnp.einsum('cri,crj->cij', grow, fall, precision=precise)]
    pallas_call x2 -> x1, Pallas kernels: 45.2 us -> 39.4 us  [reduced(): pl.pallas_call(functools.partial(reduce_kernel, devices_seq, math.gcd(wid...]
    another operation x11 -> x1, local copies, waits for them, and re-layouts: 5.32 us -> 0.15 us  [correlate_block(): entering = jnp.stack(entering[::-1], axis=2)]
    slice x3 -> x1, local copies, waits for them, and re-layouts: 3.65 us -> 0.61 us  [correlate_block(): state = sums[:, :, index] + step * state]
    dot_general x1, matrix products: 1.74 us -> 4.27 us  [local(): jnp.dot(full_grads, full_weights[:, 3 * channels:], preferred_element_typ...]
    concatenate x1 -> x0, other arithmetic: 1.99 us -> none  [local(): parts = jnp.concatenate([inward, outward], axis=1).astype(jnp.bfloat16)]
    unnamed x13 -> x25, local copies, waits for them, and re-layouts: 2 us -> 3.33 us
where the time goes in v2:
time: 127 us
  Pallas kernels  95.9 us (76%)
  matrix products  18.4 us (14%)
  local copies, waits for them, and re-layouts  9.4 us (7%)
  other arithmetic  1.97 us (2%)
    pallas_call x1, Pallas kernels, gathered(): pl.pallas_call(functools.partial(gather_kernel, devices_seq, devices_chan...  56.5 us
    pallas_call x1, Pallas kernels, reduced(): pl.pallas_call(functools.partial(reduce_kernel, devices_seq, math.gcd(wid...  39.4 us
    dot_general x1, matrix products, local(): jnp.dot(full_grads, full_weights[:, 3 * channels:], preferred_element_typ...  4.27 us
    dot_general x1, matrix products, local(): jnp.dot(full_tokens, full_weights[:, :3 * channels], preferred_element_ty...  4.25 us
    dot_general x1, matrix products, correlate_block(): taps = jnp.einsum('cri,crj->cij', grow, fall, precision=precise)  3.94 us
    dot_general x1, matrix products, correlate_block(): outer = jnp.einsum('cri,crn->cin', grow, entering, precision=precise)  3.75 us
    unnamed x25, local copies, waits for them, and re-layouts  3.33 us

profile of v2, /device:TPU:0, one launch (start us, length us, event | category | flops | bytes accessed | tf_op | source)
XLA Modules:
  0.0 126.7 jit_solution(2749694257083179361)
XLA Ops:
  0.6 1.1 copy.65
  1.7 1.0 copy.66
  2.7 0.8 pad_maximum_fusion.1.weights
  3.5 56.5 %gather_inputs.1 = (bf16[512,4096]{1,0:T(8,128)(2,1)}, bf16[512,4096]{1,0:T(8,128)(2,1)}, bf16[4096,256]{1,0:T(8,128)(2,1)}) custom-call(bf16[512,1024]{1,0:T(8,128)(2,1)} %tokens.1, bf16[512,1024]{1,0:T(8,128)(2,1)} %grads.1, bf16[512,256]{1,0:T(8,128)(2,1)} %pad_maximum_fusion.1.weights), custom_call_target="tpu_custom_call" | custom-call | tf_op jit(solution)/shard_map/gather_inputs/pallas_call | solution.py:195
  60.0 0.0 copy-start.3
  60.0 0.0 copy-start.1
  60.1 4.3 %fusion.9 = f32[512,192]{1,0:T(8,128)S(1)} fusion(bf16[512,4096]{1,0:T(8,128)(2,1)} %get-tuple-element.7.tokens_hbm, bf16[4096,256]{1,0:T(8,128)(2,1)} %get-tuple-element.6), kind=kOutput, calls=%fused_computation.12 | convolution fusion | flops 805404672 | bytes 6684672 | tf_op jit(solution)/shard_map/dot_general | solution.py:432
  64.3 0.0 copy-done.3
  64.3 0.1 copy.83
  64.4 0.0 copy-done.1
  64.4 0.0 copy-start.5
  64.5 0.0 copy-start.4
  64.5 4.3 %multiply_convert_fusion = (bf16[512,64]{1,0:T(8,128)(2,1)S(1)}, f32[512,64]{1,0:T(8,128)}, f32[512,64]{1,0:T(8,128)}, f32[512,64]{1,0:T(8,128)S(1)}, bf16[512,64]{1,0:T(8,128)(2,1)S(1)}) fusion(f32[512,64]{1,0:T(8,128)S(1)} %copy.83, f32[512,192]{1,0:T(8,128)S(1)} %fusion.9, bf16[512,4096]{1,0:T(8,128)(2,1)} %get-tuple-element.5.grads_hbm, ...), kind=kOutput, calls=%fused_computation.28 | convolution fusion | flops 268599296 | bytes 6815744 | tf_op jit(solution)/shard_map/dot_general | solution.py:435
  68.7 0.1 copy.69
  68.9 0.0 copy-done.5
  68.9 0.1 copy.59
  69.0 0.1 copy.60.rate
  69.1 0.0 copy-done.4
  69.1 0.1 copy.58
  69.2 0.1 copy.61
  69.3 0.0 copy-start.2
  69.3 0.1 copy.62
  69.4 3.9 %fusion.8 = f32[64,64,64]{1,2,0:T(8,128)S(1)} fusion(f32[64,16]{1,0:T(8,128)S(1)} %bitcast.153, f32[64,16]{1,0:T(8,128)S(1)} %copy.62, pred[64,64]{0,1:T(8,128)(4,1)S(1)} %iota_compare_fusion), kind=kOutput, calls=%fused_computation.11 | convolution fusion | flops 50855936 | bytes 1060864 | tf_op jit(solution)/shard_map/cri,crj->cij/dot_general | solution.py:408
  73.3 0.0 copy-done.2
  73.3 0.3 negate_exponential_fusion
  73.6 2.2 %fusion = f32[64,80,8]{1,2,0:T(8,128)S(1)} fusion(f32[64,16,64]{1,2,0:T(8,128)S(1)} %negate_exponential_fusion, f32[64,64,64]{1,2,0:T(8,128)S(1)} %fusion.8, f32[8,64,64]{1,0,2:T(8,128)S(1)} %copy.69), kind=kOutput, calls=%fused_computation | convolution fusion | flops 31784960 | bytes 1605632 | tf_op jit(solution)/shard_map/cij,cjn->cin/dot_general | solution.py:411
  75.8 0.6 fusion.32
  76.5 0.1 copy.100
  76.5 0.1 copy.96
  76.6 0.1 copy.99
  76.6 0.1 copy.95
  76.7 0.1 copy.98
  76.8 0.1 copy.94
  76.8 0.1 copy.97
  76.9 0.1 constant_dynamic-update-slice_fusion.7
  77.1 0.0 copy-done
  77.1 0.1 copy.80
  77.3 3.8 %fusion.13 = f32[8,64,64]{1,0,2:T(8,128)S(1)} fusion(f32[64,16,8]{1,2,0:T(8,128)S(1)} %copy.80, f32[64,16]{1,0:T(8,128)S(1)} %bitcast.155, f32[64,16]{1,0:T(8,128)S(1)} %copy.62, f32[64,80,8]{1,2,0:T(8,128)S(1)} %fusion), kind=kOutput, calls=%fused_computation.14 | convolution fusion | flops 6455296 | bytes 303104 | tf_op jit(solution)/shard_map/cri,crn->cin/dot_general | solution.py:422
  81.0 0.9 copy.81
  81.9 0.1 copy.93
  82.0 0.6 fusion.28.state
  82.6 0.7 concatenate.14.early_in
  83.3 0.8 concatenate.15.early_out
  84.0 39.4 %reduce_owned.1 = f32[2,512,128]{2,1,0:T(8,128)} custom-call(f32[16,64]{1,0:T(8,128)} %fusion.28.state, f32[16,64]{1,0:T(8,128)} %copy-done, f32[16,64]{1,0:T(8,128)} %copy-done.2, f32[512,64]{1,0:T(8,128)} %bitcast.150, f32[512,64]{1,0:T(8,128)} %get-tuple-element.23.value, f32[512,64]{1,0:T(8,128)} %get-tuple-element.22.gate, ...), custom_call_target="tpu_custom_call" | custom-call | tf_op jit(solution)/shard_map/reduce_owned/pallas_call | solution.py:380
  123.4 1.4 %slice_bitcast_fusion = (f32[512,64]{1,0:T(8,128)S(1)}, f32[512,1,64]{2,0,1:T(8,128)S(1)}, f32[512,1,64]{2,0,1:T(8,128)S(1)}, f32[512,1,64]{2,0,1:T(8,128)S(1)}) fusion(f32[2,512,128]{2,1,0:T(8,128)} %reduce_owned.1), kind=kLoop, calls=%fused_computation.24 | loop fusion | bytes 1048576 | tf_op jit(solution)/shard_map/squeeze | solution.py:464
  124.8 0.1 pad_maximum_fusion
  124.9 1.0 copy.86
  125.9 0.8 copy.87
  (13 shorter events, 0.1 us)
Async XLA Ops:
  60.0 4.3 %copy-start.3 = (bf16[512,64]{0,1:T(8,128)(2,1)S(1)}, bf16[512,64]{0,1:T(8,128)(2,1)}, u32[]{:S(2)}) copy-start(bf16[512,64]{0,1:T(8,128)(2,1)} %param.11) | copy-start | bytes 196612
  60.0 4.4 %copy-start.1 = (bf16[4096,256]{1,0:T(8,128)(2,1)S(1)}, bf16[4096,256]{1,0:T(8,128)(2,1)}, u32[]{:S(2)}) copy-start(bf16[4096,256]{1,0:T(8,128)(2,1)} %get-tuple-element.6) | copy-start | bytes 6291460
  64.4 4.5 %copy-start.5 = (f32[16,32]{1,0:T(8,128)S(1)}, f32[16,32]{1,0:T(8,128)}, u32[]{:S(2)}) copy-start(f32[16,32]{1,0:T(8,128)} %param.13) | copy-start | bytes 6148
  64.5 4.6 %copy-start.4 = (f32[16,32]{1,0:T(8,128)S(1)}, f32[16,32]{1,0:T(8,128)}, u32[]{:S(2)}) copy-start(f32[16,32]{1,0:T(8,128)} %param.12) | copy-start | bytes 6148
  69.1 8.0 %copy-start = (f32[16,64]{1,0:T(8,128)}, f32[16,64]{1,0:T(8,128)S(1)}, u32[]{:S(2)}) copy-start(f32[16,64]{1,0:T(8,128)S(1)} %copy.60.rate) | copy-start | bytes 12292
  69.3 4.1 %copy-start.2 = (f32[16,64]{1,0:T(8,128)}, f32[16,64]{1,0:T(8,128)S(1)}, u32[]{:S(2)}) copy-start(f32[16,64]{1,0:T(8,128)S(1)} %sqrt_multiply_fusion.weight) | copy-start | bytes 12292

commit v3 on v2

--- a/solution.py
+++ b/solution.py
@@ -71,10 +71,15 @@
     tokens,
     grads,
     weights,
+    tokens_out,
+    grads_out,
+    projected,
+    upstream,
     all_tokens,
     all_grads,
     all_weights,
     keep_sem,
+    store_sem,
     chan_send,
     chan_recv,
     chan_pass,
@@ -92,8 +97,8 @@
     rows = weights.shape[0]
     greet(devices_seq, devices_chan, "pairs")
 
-    def block(ref, index):
-        return ref.at[:, pl.ds(pl.multiple_of(index * columns, columns), columns)]
+    def block(ref, lines, index):
+        return ref.at[lines, pl.ds(pl.multiple_of(index * columns, columns), columns)]
 
     def piece(index):
         return all_weights.at[pl.ds(pl.multiple_of(index * rows, rows), rows)]
@@ -104,25 +109,30 @@
     def seq_member(step, parity):
         return lax.rem(seq // 2 - step + seq_groups, seq_groups) * 2 + parity
 
-    pairs = ((tokens, all_tokens), (grads, all_grads))
+    height = tokens.shape[0] // 2
+    parts = [
+        (own, whole, out, pl.ds(half * height, height))
+        for own, whole, out in ((tokens, all_tokens, tokens_out), (grads, all_grads, grads_out))
+        for half in range(2)
+    ]
 
     def chan_copy(array, step):
-        own, whole = pairs[array]
+        own, whole, _, lines = parts[array]
         there = lax.rem(chan // 2 + step, chan_groups) * 2 + chan % 2
         return remote(
-            own,
-            block(whole, chan),
+            own.at[lines],
+            block(whole, lines, chan),
             chan_send.at[array, step],
             chan_recv.at[array, step],
             (seq, there),
         )
 
     def chan_forward(array, step):
-        own, whole = pairs[array]
+        own, whole, _, lines = parts[array]
         here = chan_member(step, chan % 2)
         return remote(
-            own if step == 0 else block(whole, here),
-            block(whole, here),
+            own.at[lines] if step == 0 else block(whole, lines, here),
+            block(whole, lines, here),
             chan_pass.at[array, step],
             chan_passed.at[array, step],
             chan_pair,
@@ -145,18 +155,22 @@
 
         lax.fori_loop(1, seq_groups, body, 0)
 
-    for array in range(2):
+    def store(array):
+        _, whole, out, lines = parts[array]
+        return pltpu.make_async_copy(whole.at[lines], out.at[lines], store_sem.at[array])
+
+    for array in range(4):
         for step in range(1, chan_groups):
             chan_copy(array, step).start()
     each(lambda step: seq_copy(step).start())
     own_piece.start()
-    for array in range(2):
+    for array in range(4):
         chan_forward(array, 0).start()
-    keeps = [
-        pltpu.make_async_copy(tokens, block(all_tokens, chan), keep_sem.at[0]),
-        pltpu.make_async_copy(grads, block(all_grads, chan), keep_sem.at[1]),
-        pltpu.make_async_copy(weights, piece(seq), keep_sem.at[2]),
-    ]
+    keeps = [pltpu.make_async_copy(weights, piece(seq), keep_sem.at[4])]
+    for array, (own, whole, _, lines) in enumerate(parts):
+        keeps.append(
+            pltpu.make_async_copy(own.at[lines], block(whole, lines, chan), keep_sem.at[array])
+        )
     for keep in keeps:
         keep.start()
 
@@ -164,11 +178,13 @@
         seq_copy(step).wait_recv()
         seq_forward(step).start()
 
-    each(pass_on)
-    for array in range(2):
+    def pass_part(array):
         for step in range(1, chan_groups):
             chan_copy(array, step).wait_recv()
             chan_forward(array, step).start()
+
+    pass_part(0)
+    each(pass_on)
     for keep in keeps:
         keep.wait()
     own_piece.wait()
@@ -178,9 +194,25 @@
         seq_forward(step).wait()
 
     each(finish)
-    for array in range(2):
+    tile = math.gcd(height, 128)
+    for array, (_, whole, _, lines) in enumerate(parts):
+        if array + 1 < len(parts):
+            pass_part(array + 1)
         for step in range(chan_groups):
             chan_forward(array, step).wait()
+        store(array).start()
+        target, first = (projected, 0) if array < 2 else (upstream, all_weights.shape[1] // 2)
+
+        def product(index, carry):
+            here = pl.ds(pl.multiple_of(array % 2 * height + index * tile, tile), tile)
+            target[here] = jnp.dot(
+                whole[here], all_weights[:, first:], preferred_element_type=jnp.float32
+            )
+            return carry
+
+        lax.fori_loop(0, height // tile, product, 0)
+    for array in range(4):
+        store(array).wait()
         for step in range(1, chan_groups):
             chan_copy(array, step).wait_send()
 
@@ -194,11 +226,22 @@
     tall = jax.ShapeDtypeStruct((weights.shape[0] * devices_seq, weights.shape[1]), weights.dtype)
     return pl.pallas_call(
         functools.partial(gather_kernel, devices_seq, devices_chan),
-        out_shape=(wide, wide, tall),
+        out_shape=(
+            wide,
+            wide,
+            jax.ShapeDtypeStruct((tokens.shape[0], weights.shape[1]), jnp.float32),
+            jax.ShapeDtypeStruct((tokens.shape[0], weights.shape[1] // 2), jnp.float32),
+        ),
         in_specs=[vmem] * 3,
-        out_specs=(anywhere,) * 3,
-        scratch_shapes=[dma((3,))]
-        + [dma((2, chan_groups))] * 4
+        out_specs=(anywhere, anywhere, vmem, vmem),
+        scratch_shapes=[
+            pltpu.VMEM(wide.shape, wide.dtype),
+            pltpu.VMEM(wide.shape, wide.dtype),
+            pltpu.VMEM(tall.shape, tall.dtype),
+            dma((5,)),
+            dma((4,)),
+        ]
+        + [dma((4, chan_groups))] * 4
         + [dma((seq_groups,))] * 4,
         compiler_params=pltpu.CompilerParams(collective_id=0, has_side_effects=True),
         name="gather_inputs",
@@ -428,13 +471,9 @@
     channels = out_weight.shape[1]
     owned_rows = in_weight.shape[0]
     weights = jnp.concatenate([in_weight.reshape(owned_rows, 3 * channels), out_weight], axis=1)
-    full_tokens, full_grads, full_weights = gathered(tokens, grad_out, weights)
-    projected = jnp.dot(
-        full_tokens, full_weights[:, : 3 * channels], preferred_element_type=jnp.float32
-    )
-    upstream = jnp.dot(
-        full_grads, full_weights[:, 3 * channels :], preferred_element_type=jnp.float32
-    )
+    full_tokens, full_grads, projected, upstream = gathered(tokens, grad_out, weights)
+    projected = projected[:, : 3 * channels]
+    upstream = upstream[:, channels:]
     streams = lax.reduce_precision(projected, exponent_bits=8, mantissa_bits=7)
     gate_first = streams[:, :channels]
     gate_second = streams[:, channels : 2 * channels]

time: 127 us -> 122 us (0.961)
  matrix products: 18.4 us -> 9.75 us
  other arithmetic: 1.97 us -> 5.7 us
  Pallas kernels: 95.9 us -> 97.2 us
    dot_general x2 -> x0, matrix products: 8.52 us -> none  [the longest x1 4.27 us: local(): jnp.dot(full_grads, full_weights[:, 3 * channels:], preferred_element_typ...]
    convert_element_type x0 -> x1, other arithmetic: none -> 1.95 us  [local(): gated = (gate_second * conv_value).astype(jnp.bfloat16)]
    unnamed x25 -> x24, local copies, waits for them, and re-layouts: 3.33 us -> 3.31 us
where the time goes in v3:
time: 122 us
  Pallas kernels  97.2 us (80%)
  matrix products  9.75 us (8%)
  local copies, waits for them, and re-layouts  8.36 us (7%)
  other arithmetic  5.7 us (5%)
    pallas_call x1, Pallas kernels, gathered(): pl.pallas_call(functools.partial(gather_kernel, devices_seq, devices_chan...  57.8 us
    pallas_call x1, Pallas kernels, reduced(): pl.pallas_call(functools.partial(reduce_kernel, devices_seq, math.gcd(wid...  39.4 us
    dot_general x1, matrix products, correlate_block(): taps = jnp.einsum('cri,crj->cij', grow, fall, precision=precise)  3.95 us
    dot_general x1, matrix products, correlate_block(): outer = jnp.einsum('cri,crn->cin', grow, entering, precision=precise)  3.58 us
    unnamed x24, local copies, waits for them, and re-layouts  3.31 us

profile of v3, /device:TPU:0, one launch (start us, length us, event | category | flops | bytes accessed | tf_op | source)
XLA Modules:
  0.0 122.0 jit_solution(4295196529357408342)
XLA Ops:
  0.6 0.7 broadcast_divide_fusion
  1.3 0.1 copy.29
  1.4 0.1 copy.30.rate
  1.5 0.0 copy-start
  1.5 0.8 copy.28
  2.3 0.1 copy.31
  2.4 0.0 copy-start.2
  2.4 0.1 copy.32
  2.5 0.0 copy-start.1
  2.5 0.0 copy-start.3
  2.5 4.0 %fusion.6 = f32[64,64,64]{1,2,0:T(8,128)S(1)} fusion(f32[64,16]{1,0:T(8,128)S(1)} %bitcast.151, f32[64,16]{1,0:T(8,128)S(1)} %copy.32, pred[64,64]{0,1:T(8,128)(4,1)S(1)} %iota_compare_fusion), kind=kOutput, calls=%fused_computation.9 | convolution fusion | flops 50855936 | bytes 1060864 | tf_op jit(solution)/shard_map/cri,crj->cij/dot_general | solution.py:451
  6.5 0.0 copy-done.2
  6.5 0.0 copy-done.1
  6.5 0.1 copy.33
  6.6 0.0 copy-done.3
  6.7 0.0 copy-start.4
  6.7 0.1 copy.34
  6.8 0.8 pad_maximum_fusion.1.weights
  7.6 57.8 %gather_inputs.1 = (bf16[512,4096]{1,0:T(8,128)(2,1)}, bf16[512,4096]{1,0:T(8,128)(2,1)}, f32[512,256]{1,0:T(8,128)}, f32[512,128]{1,0:T(8,128)}) custom-call(bf16[512,1024]{1,0:T(8,128)(2,1)} %tokens.1, bf16[512,1024]{1,0:T(8,128)(2,1)} %grads.1, bf16[512,256]{1,0:T(8,128)(2,1)} %pad_maximum_fusion.1.weights), custom_call_target="tpu_custom_call" | custom-call | tf_op jit(solution)/shard_map/gather_inputs/pallas_call | solution.py:227
  65.4 1.1 slice_reduce-precision_fusion
  66.5 0.0 copy-done.4
  66.5 0.1 copy.48
  66.6 1.9 %fusion.14 = (bf16[512,64]{1,0:T(8,128)(2,1)S(1)}, f32[512,64]{1,0:T(8,128)}, f32[512,64]{1,0:T(8,128)}, f32[512,64]{1,0:T(8,128)S(1)}, bf16[512,64]{1,0:T(8,128)(2,1)S(1)}) fusion(bf16[512,64]{1,0:T(8,128)(2,1)S(1)} %copy.48, f32[512,192]{1,0:T(8,128)S(1)} %slice_reduce-precision_fusion, f32[512,128]{1,0:T(8,128)} %get-tuple-element.6), kind=kLoop, calls=%fused_computation.21 | loop fusion | flops 196608 | bytes 1114112 | tf_op jit(solution)/shard_map/convert_element_type | solution.py:482
  68.6 0.1 copy.35
  68.7 0.3 negate_exponential_fusion
  69.0 2.2 %fusion = f32[64,80,8]{1,2,0:T(8,128)S(1)} fusion(f32[64,16,64]{1,2,0:T(8,128)S(1)} %negate_exponential_fusion, f32[64,64,64]{1,2,0:T(8,128)S(1)} %fusion.6, f32[8,64,64]{1,0,2:T(8,128)S(1)} %copy.35), kind=kOutput, calls=%fused_computation | convolution fusion | flops 31784960 | bytes 1605632 | tf_op jit(solution)/shard_map/cij,cjn->cin/dot_general | solution.py:454
  71.3 0.6 fusion.27
  71.9 0.1 copy.60
  71.9 0.1 copy.56
  72.0 0.1 copy.59
  72.1 0.1 copy.55
  72.1 0.1 copy.58
  72.2 0.1 copy.54
  72.2 0.1 copy.57
  72.3 0.1 constant_dynamic-update-slice_fusion.7
  72.5 0.0 copy-done
  72.5 0.1 copy.46
  72.7 3.6 %fusion.8 = f32[8,64,64]{1,0,2:T(8,128)S(1)} fusion(f32[64,16,8]{1,2,0:T(8,128)S(1)} %copy.46, f32[64,16]{1,0:T(8,128)S(1)} %bitcast.153, f32[64,16]{1,0:T(8,128)S(1)} %copy.32, f32[64,80,8]{1,2,0:T(8,128)S(1)} %fusion), kind=kOutput, calls=%fused_computation.11 | convolution fusion | flops 6455296 | bytes 303104 | tf_op jit(solution)/shard_map/cri,crn->cin/dot_general | solution.py:465
  76.3 0.9 copy.47
  77.1 0.1 copy.53
  77.2 0.6 fusion.23.state
  77.8 0.7 concatenate.14.early_in
  78.5 0.8 concatenate.15.early_out
  79.3 39.4 %reduce_owned.1 = f32[2,512,128]{2,1,0:T(8,128)} custom-call(f32[16,64]{1,0:T(8,128)} %fusion.23.state, f32[16,64]{1,0:T(8,128)} %copy-done, f32[16,64]{1,0:T(8,128)} %copy-done.2, f32[512,64]{1,0:T(8,128)} %bitcast.148, f32[512,64]{1,0:T(8,128)} %get-tuple-element.23.value, f32[512,64]{1,0:T(8,128)} %get-tuple-element.22.gate, ...), custom_call_target="tpu_custom_call" | custom-call | tf_op jit(solution)/shard_map/reduce_owned/pallas_call | solution.py:423
  118.7 1.4 %slice_bitcast_fusion = (f32[512,64]{1,0:T(8,128)S(1)}, f32[512,1,64]{2,0,1:T(8,128)S(1)}, f32[512,1,64]{2,0,1:T(8,128)S(1)}, f32[512,1,64]{2,0,1:T(8,128)S(1)}) fusion(f32[2,512,128]{2,1,0:T(8,128)} %reduce_owned.1), kind=kLoop, calls=%fused_computation.24 | loop fusion | bytes 1048576 | tf_op jit(solution)/shard_map/squeeze | solution.py:503
  120.1 0.1 pad_maximum_fusion
  120.2 1.0 copy.50
  121.2 0.8 copy.51
  (11 shorter events, 0.1 us)
Async XLA Ops:
  1.5 71.0 %copy-start = (f32[16,64]{1,0:T(8,128)}, f32[16,64]{1,0:T(8,128)S(1)}, u32[]{:S(2)}) copy-start(f32[16,64]{1,0:T(8,128)S(1)} %copy.30.rate) | copy-start | bytes 12292
  2.4 4.1 %copy-start.2 = (f32[16,64]{1,0:T(8,128)}, f32[16,64]{1,0:T(8,128)S(1)}, u32[]{:S(2)}) copy-start(f32[16,64]{1,0:T(8,128)S(1)} %sqrt_multiply_fusion.weight) | copy-start | bytes 12292
  2.5 4.0 %copy-start.1 = (bf16[512,3,64]{0,2,1:T(8,128)(2,1)S(1)}, bf16[512,3,64]{0,2,1:T(8,128)(2,1)}, u32[]{:S(2)}) copy-start(bf16[512,3,64]{0,2,1:T(8,128)(2,1)} %param.9) | copy-start | bytes 589828
  2.5 4.1 %copy-start.3 = (bf16[512,64]{0,1:T(8,128)(2,1)S(1)}, bf16[512,64]{0,1:T(8,128)(2,1)}, u32[]{:S(2)}) copy-start(bf16[512,64]{0,1:T(8,128)(2,1)} %param.10) | copy-start | bytes 196612
  6.7 59.9 %copy-start.4 = (bf16[512,64]{0,1:T(8,128)(2,1)S(1)}, bf16[512,64]{0,1:T(8,128)(2,1)}, u32[]{:S(2)}) copy-start(bf16[512,64]{0,1:T(8,128)(2,1)} %param.11) | copy-start | bytes 196612
